TPU v7x, 32 devices: a whole 2x2x4 slice. The times are simulated.
32 devices in a mesh: act: 4 (over x, core), fld: 8 (over z, y).
Axes of the slice: x: 2, y: 2, z: 4, core: 2. Of those that a mesh axis runs over, the one named last changes fastest.
Arguments:
- star_state: float32 [12, 32768], P(None, 'fld'), may hold values from -12 to 12
- star_times: float32 [32768], P('fld'), may hold values from -0.25 to 0
- masses: float32 [32768], P('fld'), may hold values from 6.1035155e-07 to 1.5258789e-05
- active_ids: int32 [4, 2048], replicated, may hold values from 0 to 32767, as said below
Outputs:
- final_state: float32 [12, 32768], P(None, 'fld')
- active_potentials: float32 [4, 2048], P(None, 'act')
Inputs may be any that keep to these rules, and one draw needn't show every extreme that they name: `active_ids`: each row lists 2048 distinct star indices; the owners of the listed stars are uneven, with many listed stars in a few blocks of 4096 consecutive indices.
All inputs are finite; a program needn't handle non-finite values.
Results may differ from a plain program's by a relative error of at most 0.0001.
Values sent between devices are 32-bit elements; how exact they have to be, the bound alone decides.
A program may use at most 64 MiB of HBM per device.

v0:
```python
import jax
import jax.numpy as jnp
from jax import lax
from jax.sharding import PartitionSpec as P

soften_square = 0.01
block_step = 0.0625


def predict(current, delta):
    position = current[0:3]
    velocity = current[3:6]
    acceleration = current[6:9]
    jerk_rows = current[9:12]
    new_position = position + delta * (
        velocity + delta * (acceleration / 2.0 + delta * jerk_rows / 6.0)
    )
    new_velocity = velocity + delta * (acceleration + delta * jerk_rows / 2.0)
    return (new_position, new_velocity)


def pair_sums(active_pos, active_vel, field_pos, field_vel, field_mass):
    field_count = field_pos.shape[1]
    block_width = min(field_count, 1024)
    block_turns = field_count // block_width

    def one_block(turn_index, carried):
        block_start = turn_index * block_width
        block_pos = lax.dynamic_slice_in_dim(field_pos, block_start, block_width, 1)
        block_vel = lax.dynamic_slice_in_dim(field_vel, block_start, block_width, 1)
        block_mass = lax.dynamic_slice_in_dim(field_mass, block_start, block_width, 0)
        separation = block_pos[:, None, :] - active_pos[:, :, None]
        rel_vel = block_vel[:, None, :] - active_vel[:, :, None]
        soft_square = jnp.sum(separation * separation, axis=0) + soften_square
        inverse = 1.0 / jnp.sqrt(soft_square)
        weights = block_mass[None, :] * inverse * inverse * inverse
        radial = jnp.sum(separation * rel_vel, axis=0)
        pull = jnp.sum(weights * separation, axis=-1)
        jerk_sum = jnp.sum(weights * (rel_vel - 3.0 * (radial / soft_square) * separation), axis=-1)
        potential = -jnp.sum(block_mass[None, :] * inverse, axis=-1)
        return carried + jnp.concatenate([pull, jerk_sum, potential[None]], 0)

    start_value = jnp.zeros((7, active_pos.shape[1]), jnp.float32)
    return lax.fori_loop(0, block_turns, one_block, start_value)


def correct(previous, pair_terms, elapsed):
    old_pos = previous[0:3]
    old_vel = previous[3:6]
    old_acc = previous[6:9]
    old_jerk = previous[9:12]
    new_acc = pair_terms[0:3]
    new_jerk = pair_terms[3:6]
    new_vel = (
        old_vel
        + elapsed * (old_acc + new_acc) / 2.0
        + elapsed * elapsed * (old_jerk - new_jerk) / 12.0
    )
    new_pos = (
        old_pos
        + elapsed * (old_vel + new_vel) / 2.0
        + elapsed * elapsed * (old_acc - new_acc) / 12.0
    )
    return jnp.concatenate([new_pos, new_vel, new_acc, new_jerk], 0)


def body(star_state, star_times, masses, active_ids):
    field_count = star_state.shape[1]
    first_star = lax.axis_index("fld") * field_count
    block_size = active_ids.shape[1] // lax.axis_size("act")
    act_index = lax.axis_index("act")
    current = star_state
    star_clock = star_times
    potential_rows = []
    history = []
    my_lists = lax.dynamic_slice_in_dim(active_ids, act_index * block_size, block_size, 1)
    rows_all = my_lists - first_star
    owned_all = (rows_all >= 0) & (rows_all < field_count)
    safe_all = jnp.clip(rows_all, 0, field_count - 1)
    picked_all = jnp.concatenate([star_state[:, safe_all], star_times[safe_all][None]], 0)
    picked_all = picked_all * owned_all[None].astype(jnp.float32)
    fetched = lax.psum(picked_all, "fld")
    for step_index in range(active_ids.shape[0]):
        now_time = (step_index + 1) * block_step
        field_pos, field_vel = predict(current, now_time - star_clock)
        block_ids = lax.dynamic_slice_in_dim(
            active_ids[step_index], act_index * block_size, block_size, 0
        )
        previous = fetched[:, step_index]
        for earlier in range(step_index):
            matched = (block_ids[:, None] == active_ids[earlier][None, :]).astype(jnp.float32)
            carried_rows = jnp.dot(
                history[earlier],
                matched.T,
                precision=lax.Precision.HIGHEST,
                preferred_element_type=jnp.float32,
            )
            earlier_time = jnp.full((1, block_size), (earlier + 1) * block_step, jnp.float32)
            seen_before = jnp.sum(matched, axis=1) > 0.5
            replaced = jnp.concatenate([carried_rows, earlier_time], 0)
            previous = jnp.where(seen_before[None], replaced, previous)
        elapsed = now_time - previous[12]
        active_pos, active_vel = predict(previous[:12], elapsed)
        pair_terms = pair_sums(active_pos, active_vel, field_pos, field_vel, masses)
        totals = lax.psum(pair_terms, "fld")
        refreshed = correct(previous[:12], totals, elapsed)
        potential_rows.append(totals[6])
        updates = lax.all_gather(refreshed, "act", axis=1, tiled=True)
        history.append(updates)
        list_rows = active_ids[step_index] - first_star
        list_owned = (list_rows >= 0) & (list_rows < field_count)
        target_rows = jnp.where(list_owned, list_rows, field_count)
        current = current.at[:, target_rows].set(updates, mode="drop")
        star_clock = star_clock.at[target_rows].set(now_time, mode="drop")
    return (current, jnp.stack(potential_rows, 0))


def solution(mesh):
    in_specs = (P(None, "fld"), P("fld"), P("fld"), P())
    out_specs = (P(None, "fld"), P(None, "act"))
    return jax.shard_map(body, mesh=mesh, in_specs=in_specs, out_specs=out_specs, check_vma=False)
```

profile of v0, /device:TPU:0, one launch (start us, length us, event | category | flops | bytes accessed | tf_op | source)
XLA Modules:
  0.0 446.7 jit_solution(1028361235867738751)
XLA Ops:
  11.5 20.6 %gather_fusion.1 = f32[2048]{0:T(1024)} fusion(f32[4096]{0:T(1024)S(1)} %copy.175, s32[2048]{0:T(1024)S(1)} %broadcast_clamp_fusion), kind=kCustom, calls=%fused_computation.1 | custom fusion | bytes 24576 | tf_op jit(solution)/shard_map/gather | solution.py:80
  32.1 5.5 %gather_fusion = f32[2048,12]{1,0:T(8,128)S(1)} fusion(f32[12,4096]{0,1:T(8,128)S(1)} %copy.109, s32[2048]{0:T(1024)S(1)} %broadcast_clamp_fusion), kind=kCustom, calls=%fused_computation | custom fusion | bytes 204800 | tf_op jit(solution)/shard_map/gather | solution.py:80
  41.4 8.1 %scatter_fusion.1 = f32[4096]{0:T(1024)S(1)} fusion(f32[4096]{0:T(1024)S(1)} %copy.175, s32[2048]{0:T(1024)S(1)} %bitcast.139, f32[2048]{0:T(1024)S(1)} %broadcast.532), kind=kCustom, calls=%fused_computation.3 | custom fusion | bytes 32768 | tf_op jit(solution)/shard_map/scatter | solution.py:114
  50.1 8.1 %scatter_fusion.3 = f32[4096]{0:T(1024)S(1)} fusion(f32[4096]{0:T(1024)S(1)} %scatter_fusion.1, s32[2048]{0:T(1024)S(1)} %bitcast.137, f32[2048]{0:T(1024)S(1)} %broadcast.533), kind=kCustom, calls=%fused_computation.5 | custom fusion | bytes 32768 | tf_op jit(solution)/shard_map/scatter | solution.py:114
  58.7 8.1 %scatter_fusion.5 = f32[4096]{0:T(1024)S(1)} fusion(f32[4096]{0:T(1024)S(1)} %scatter_fusion.3, s32[2048]{0:T(1024)S(1)} %bitcast.135, f32[2048]{0:T(1024)S(1)} %broadcast.534), kind=kCustom, calls=%fused_computation.7 | custom fusion | bytes 32768 | tf_op jit(solution)/shard_map/scatter | solution.py:114
  72.9 39.6 %all-reduce.8.cloned.1.call-done = f32[13,4,512]{2,0,1:T(8,128)} async-done(((f32[13,4,512]{2,0,1:T(8,128)}), f32[13,4,512]{2,0,1:T(8,128)}) %all-reduce.8.cloned.1.call-update) | async-done | bytes 106512 | tf_op jit(solution)/shard_map/psum | solution.py:82
  114.2 20.4 %while.56 = (s32[]{:T(128)}, f32[7,512]{1,0:T(8,128)S(1)}, f32[3,4096]{1,0:T(4,128)S(1)}, f32[3,512]{1,0:T(4,128)S(1)}, f32[4096]{0:T(1024)S(1)}, /*index=5*/f32...) while((s32[]{:T(128)}, f32[7,512]{1,0:T(8,128)S(1)}, ...), condition=%wide.region_7.8_spmd.clone, body=%wide.region_1.7_spmd.clone.sunk | while | flops 24652804 | bytes 16974004 | solution.py:44
  134.5 35.3 %psum.36 = f32[7,512]{1,0:T(8,128)S(1)} all-reduce(f32[7,512]{1,0:T(8,128)S(1)} %get-tuple-element.498), channel_id=1, replica_groups=mesh['act'=4,'fld'=8] {'fld'}, use_global_device_ids=true, to_apply=%region_8.9 | all-reduce | flops 3584 | bytes 28672 | tf_op jit(solution)/shard_map/psum | solution.py:105
  170.5 5.6 %all_gather.12 = f32[12,2048]{1,0:T(8,128)S(1)} all-gather(f32[12,512]{1,0:T(8,128)S(1)} %pad_maximum_fusion), channel_id=1, replica_groups=mesh['act'=4,'fld'=8] {'act'}, dimensions={1}, use_global_device_ids=true | all-gather | bytes 122880 | tf_op jit(solution)/shard_map/all_gather | solution.py:108
  184.5 6.4 %scatter_fusion = f32[12,4096]{0,1:T(8,128)S(1)} fusion(f32[12,4096]{0,1:T(8,128)S(1)} %copy.109, s32[2048]{0:T(1024)S(1)} %bitcast.140, f32[2048,12]{1,0:T(8,128)S(1)} %copy.110), kind=kCustom, calls=%fused_computation.2 | custom fusion | bytes 303104 | tf_op jit(solution)/shard_map/scatter | solution.py:113
  190.9 4.9 %fusion.79 = (f32[3,4096]{0,1:T(8,128)}, f32[3,4096]{0,1:T(8,128)}, f32[3,4096]{0,1:T(8,128)}, f32[3,4096]{0,1:T(8,128)}) fusion(f32[12,4096]{0,1:T(8,128)S(1)} %scatter_fusion), kind=kLoop, calls=%fused_computation.204 | loop fusion | bytes 393216 | tf_op jit(solution)/shard_map/slice | solution.py:14
  204.8 20.4 %while.57 = (s32[]{:T(128)}, f32[7,512]{1,0:T(8,128)S(1)}, f32[3,4096]{1,0:T(4,128)S(1)}, f32[3,512]{1,0:T(4,128)S(1)}, f32[4096]{0:T(1024)S(1)}, /*index=5*/f32...) while((s32[]{:T(128)}, f32[7,512]{1,0:T(8,128)S(1)}, ...), condition=%wide.region_18.19_spmd.clone, body=%wide.region_12.18_spmd.clone.sunk | while | flops 24652804 | bytes 16974004 | solution.py:44
  225.2 33.0 %psum.37 = f32[7,512]{1,0:T(8,128)S(1)} all-reduce(f32[7,512]{1,0:T(8,128)S(1)} %get-tuple-element.499), channel_id=1, replica_groups=mesh['act'=4,'fld'=8] {'fld'}, use_global_device_ids=true, to_apply=%region_19.20 | all-reduce | flops 3584 | bytes 28672 | tf_op jit(solution)/shard_map/psum | solution.py:105
  258.8 5.6 %all_gather.13 = f32[12,2048]{1,0:T(8,128)S(1)} all-gather(f32[12,512]{1,0:T(8,128)S(1)} %pad_maximum_fusion.1), channel_id=1, replica_groups=mesh['act'=4,'fld'=8] {'act'}, dimensions={1}, use_global_device_ids=true | all-gather | bytes 122880 | tf_op jit(solution)/shard_map/all_gather | solution.py:108
  269.3 6.4 %scatter_fusion.2 = f32[12,4096]{0,1:T(8,128)S(1)} fusion(f32[12,4096]{0,1:T(8,128)S(1)} %scatter_fusion, s32[2048]{0:T(1024)S(1)} %bitcast.138, f32[2048,12]{1,0:T(8,128)S(1)} %copy.115), kind=kCustom, calls=%fused_computation.4 | custom fusion | bytes 303104 | tf_op jit(solution)/shard_map/scatter | solution.py:113
  275.7 4.9 %fusion.78 = (f32[3,4096]{0,1:T(8,128)}, f32[3,4096]{0,1:T(8,128)}, f32[3,4096]{0,1:T(8,128)}, f32[3,4096]{0,1:T(8,128)}) fusion(f32[12,4096]{0,1:T(8,128)S(1)} %scatter_fusion.2), kind=kLoop, calls=%fused_computation.203 | loop fusion | bytes 393216 | tf_op jit(solution)/shard_map/slice | solution.py:14
  289.6 20.4 %while.58 = (s32[]{:T(128)}, f32[7,512]{1,0:T(8,128)S(1)}, f32[3,4096]{1,0:T(4,128)S(1)}, f32[3,512]{1,0:T(4,128)S(1)}, f32[4096]{0:T(1024)S(1)}, /*index=5*/f32...) while((s32[]{:T(128)}, f32[7,512]{1,0:T(8,128)S(1)}, ...), condition=%wide.region_30.31_spmd.clone, body=%wide.region_24.30_spmd.clone.sunk | while | flops 24652804 | bytes 16974004 | solution.py:44
  310.0 33.0 %psum.38 = f32[7,512]{1,0:T(8,128)S(1)} all-reduce(f32[7,512]{1,0:T(8,128)S(1)} %get-tuple-element.500), channel_id=1, replica_groups=mesh['act'=4,'fld'=8] {'fld'}, use_global_device_ids=true, to_apply=%region_31.32 | all-reduce | flops 3584 | bytes 28672 | tf_op jit(solution)/shard_map/psum | solution.py:105
  343.6 5.4 %all_gather.14 = f32[12,2048]{1,0:T(8,128)S(1)} all-gather(f32[12,512]{1,0:T(8,128)S(1)} %pad_maximum_fusion.2), channel_id=1, replica_groups=mesh['act'=4,'fld'=8] {'act'}, dimensions={1}, use_global_device_ids=true | all-gather | bytes 122880 | tf_op jit(solution)/shard_map/all_gather | solution.py:108
  351.4 6.6 %scatter_fusion.4 = f32[12,4096]{0,1:T(8,128)S(1)} fusion(f32[12,4096]{0,1:T(8,128)S(1)} %scatter_fusion.2, s32[2048]{0:T(1024)S(1)} %bitcast.136, f32[2048,12]{1,0:T(8,128)S(1)} %copy.120), kind=kCustom, calls=%fused_computation.6 | custom fusion | bytes 303104 | tf_op jit(solution)/shard_map/scatter | solution.py:113
  371.9 20.4 %while.59 = (s32[]{:T(128)}, f32[7,512]{1,0:T(8,128)S(1)}, f32[3,4096]{1,0:T(4,128)S(1)}, f32[3,512]{1,0:T(4,128)S(1)}, f32[4096]{0:T(1024)S(1)}, /*index=5*/f32...) while((s32[]{:T(128)}, f32[7,512]{1,0:T(8,128)S(1)}, ...), condition=%wide.region_43.44_spmd.clone, body=%wide.region_37.43_spmd.clone.sunk | while | flops 24652804 | bytes 16974004 | solution.py:44
  392.2 33.0 %psum.39 = f32[7,512]{1,0:T(8,128)S(1)} all-reduce(f32[7,512]{1,0:T(8,128)S(1)} %get-tuple-element.501), channel_id=1, replica_groups=mesh['act'=4,'fld'=8] {'fld'}, use_global_device_ids=true, to_apply=%region_44.45 | all-reduce | flops 3584 | bytes 28672 | tf_op jit(solution)/shard_map/psum | solution.py:105
  425.3 5.4 %all_gather.15 = f32[12,2048]{1,0:T(8,128)S(1)} all-gather(f32[12,512]{1,0:T(8,128)S(1)} %pad_maximum_fusion.3), channel_id=1, replica_groups=mesh['act'=4,'fld'=8] {'act'}, dimensions={1}, use_global_device_ids=true | all-gather | bytes 122880 | tf_op jit(solution)/shard_map/all_gather | solution.py:108
  431.1 6.4 %scatter_fusion.6 = f32[12,4096]{0,1:T(8,128)S(1)} fusion(f32[12,4096]{0,1:T(8,128)S(1)} %scatter_fusion.4, s32[2048]{0:T(1024)S(1)} %bitcast.145, f32[2048,12]{1,0:T(8,128)S(1)} %copy.125), kind=kCustom, calls=%fused_computation.8 | custom fusion | bytes 303104 | tf_op jit(solution)/shard_map/scatter | solution.py:113
  (255 shorter events, 149.0 us)
Async XLA Ops:
  7.2 105.4 %all-reduce.8.cloned.1.call-start = ((), (), s32[]{:S(2)}) async-start(), calls=%async_computation | async-start | bytes 262144 | tf_op jit(solution)/shard_map/psum | solution.py:82
  32.1 9.2 %copy-start = (f32[12,4096]{1,0:T(8,128)S(1)}, f32[12,4096]{1,0:T(8,128)}, u32[]{:S(2)}) copy-start(f32[12,4096]{1,0:T(8,128)} %param.12) | copy-start | bytes 589828
  41.3 26.2 %copy-start.11 = (s32[1,2048]{1,0:T(1,128)}, s32[1,2048]{1,0:T(1,128)S(1)}, u32[]{:S(2)}) copy-start(s32[1,2048]{1,0:T(1,128)S(1)} %get-tuple-element.773) | copy-start | bytes 24580
  41.3 26.2 %copy-start.13 = (s32[1,2048]{1,0:T(1,128)}, s32[1,2048]{1,0:T(1,128)S(1)}, u32[]{:S(2)}) copy-start(s32[1,2048]{1,0:T(1,128)S(1)} %get-tuple-element.774) | copy-start | bytes 24580
  58.7 55.4 %copy-start.1 = (f32[4096]{0:T(1024)S(1)}, f32[4096]{0:T(1024)}, u32[]{:S(2)}) copy-start(f32[4096]{0:T(1024)} %param.14) | copy-start | bytes 49156
  67.4 110.5 %copy-start.24 = (s32[1,512]{1,0:T(1,128)}, s32[1,512]{1,0:T(1,128)S(1)}, u32[]{:S(2)}) copy-start(s32[1,512]{1,0:T(1,128)S(1)} %get-tuple-element.777) | copy-start | bytes 6148
  67.4 113.0 %copy-start.27 = (s32[1,512]{1,0:T(1,128)}, s32[1,512]{1,0:T(1,128)S(1)}, u32[]{:S(2)}) copy-start(s32[1,512]{1,0:T(1,128)S(1)} %get-tuple-element.778) | copy-start | bytes 6148
  114.1 56.3 %copy-start.2 = (f32[13,4,512]{2,0,1:T(8,128)S(1)}, f32[13,4,512]{2,0,1:T(8,128)}, u32[]{:S(2)}) copy-start(f32[13,4,512]{2,0,1:T(8,128)} %all-reduce.8.cloned.1.call-done) | copy-start | bytes 319492
  204.7 54.0 %copy-start.10 = (f32[1,512]{1,0:T(1,128)S(1)}, f32[1,512]{1,0:T(1,128)}, u32[]{:S(2)}) copy-start(f32[1,512]{1,0:T(1,128)} %copy-done.9) | copy-start | bytes 6148
  204.8 54.0 %copy-start.15 = (f32[1,512]{1,0:T(1,128)S(1)}, f32[1,512]{1,0:T(1,128)}, u32[]{:S(2)}) copy-start(f32[1,512]{1,0:T(1,128)} %get-tuple-element.771) | copy-start | bytes 6148
  204.8 59.7 %copy-start.14 = (s32[1,2048]{1,0:T(1,128)S(1)}, s32[1,2048]{1,0:T(1,128)}, u32[]{:S(2)}) copy-start(s32[1,2048]{1,0:T(1,128)} %copy-done.13) | copy-start | bytes 24580
  204.8 59.7 %copy-start.28 = (s32[1,512]{1,0:T(1,128)S(1)}, s32[1,512]{1,0:T(1,128)}, u32[]{:S(2)}) copy-start(s32[1,512]{1,0:T(1,128)} %copy-done.27) | copy-start | bytes 6148
  204.8 61.5 %copy-start.25 = (s32[1,512]{1,0:T(1,128)S(1)}, s32[1,512]{1,0:T(1,128)}, u32[]{:S(2)}) copy-start(s32[1,512]{1,0:T(1,128)} %copy-done.24) | copy-start | bytes 6148
  225.2 43.7 %copy-start.8 = (f32[12,512]{1,0:T(8,128)S(1)}, f32[12,512]{1,0:T(8,128)}, u32[]{:S(2)}) copy-start(f32[12,512]{1,0:T(8,128)} %fusion.26) | copy-start | bytes 73732
  225.2 43.7 %copy-start.22 = (pred[512]{0:T(512)(128)(4,1)S(1)}, pred[512]{0:T(512)(128)(4,1)}, u32[]{:S(2)}) copy-start(pred[512]{0:T(512)(128)(4,1)} %broadcast_compare_fusion.3) | copy-start | bytes 1540
  225.2 43.7 %copy-start.23 = (pred[512]{0:T(512)(128)(4,1)S(1)}, pred[512]{0:T(512)(128)(4,1)}, u32[]{:S(2)}) copy-start(pred[512]{0:T(512)(128)(4,1)} %broadcast_compare_fusion.4) | copy-start | bytes 1540
  289.5 59.5 %copy-start.12 = (s32[1,2048]{1,0:T(1,128)S(1)}, s32[1,2048]{1,0:T(1,128)}, u32[]{:S(2)}) copy-start(s32[1,2048]{1,0:T(1,128)} %copy-done.11) | copy-start | bytes 24580
  289.5 59.5 %copy-start.26 = (s32[1,512]{1,0:T(1,128)S(1)}, s32[1,512]{1,0:T(1,128)}, u32[]{:S(2)}) copy-start(s32[1,512]{1,0:T(1,128)} %copy-done.24) | copy-start | bytes 6148
  289.6 61.3 %copy-start.6 = (f32[12,512]{1,0:T(8,128)S(1)}, f32[12,512]{1,0:T(8,128)}, u32[]{:S(2)}) copy-start(f32[12,512]{1,0:T(8,128)} %fusion.20) | copy-start | bytes 73732
  289.6 61.3 %copy-start.7 = (f32[12,512]{1,0:T(8,128)S(1)}, f32[12,512]{1,0:T(8,128)}, u32[]{:S(2)}) copy-start(f32[12,512]{1,0:T(8,128)} %fusion.22) | copy-start | bytes 73732
  289.6 61.3 %copy-start.19 = (pred[512]{0:T(512)(128)(4,1)S(1)}, pred[512]{0:T(512)(128)(4,1)}, u32[]{:S(2)}) copy-start(pred[512]{0:T(512)(128)(4,1)} %broadcast_compare_fusion) | copy-start | bytes 1540
  289.6 61.3 %copy-start.20 = (pred[512]{0:T(512)(128)(4,1)S(1)}, pred[512]{0:T(512)(128)(4,1)}, u32[]{:S(2)}) copy-start(pred[512]{0:T(512)(128)(4,1)} %broadcast_compare_fusion.1) | copy-start | bytes 1540
  289.6 61.3 %copy-start.21 = (pred[512]{0:T(512)(128)(4,1)S(1)}, pred[512]{0:T(512)(128)(4,1)}, u32[]{:S(2)}) copy-start(pred[512]{0:T(512)(128)(4,1)} %broadcast_compare_fusion.2) | copy-start | bytes 1540
  431.1 7.7 %copy-start.16 = (f32[1,512]{1,0:T(1,128)S(1)}, f32[1,512]{1,0:T(1,128)}, u32[]{:S(2)}) copy-start(f32[1,512]{1,0:T(1,128)} %slice.357) | copy-start | bytes 6148
  (6 other events, 29.4 us)
Sparse Core Ops, SparseCore 0:
  39.4 73.0 all-reduce.7
where the time goes:
time: 455 us; the launch traced here: 447 us
  blocking collectives  156 us (34%)
  local copies, waits for them, and re-layouts  126 us (28%)
  other arithmetic  95 us (21%)
  waiting for transfers between devices  39.7 us (9%)
  between operations  15 us (3%)
  matrix products  13.2 us (3%)
    psum x4, blocking collectives, body(): totals = lax.psum(pair_terms, 'fld')  134 us
    psum x1, waiting for transfers between devices, body(): fetched = lax.psum(picked_all, 'fld')  39.6 us
    reduce_sum x16, other arithmetic, one_block(): pull = jnp.sum(weights * separation, axis=-1)  38.9 us
    unnamed x74, local copies, waits for them, and re-layouts  31 us
    reduce_sum x16, other arithmetic, one_block(): radial = jnp.sum(separation * rel_vel, axis=0)  28.6 us
    scatter x4, local copies, waits for them, and re-layouts, body(): current = current.at[:, target_rows].set(updates, mode='drop')  25.7 us
    scatter x3, local copies, waits for them, and re-layouts, body(): star_clock = star_clock.at[target_rows].set(now_time, mode='drop')  24.2 us
    all_gather x4, blocking collectives, body(): updates = lax.all_gather(refreshed, 'act', axis=1, tiled=True)  22.1 us
  transfers between devices with their start and end apart: 1, of which 1 were waited for; matrix products, arithmetic and copies ran while one was open for 7% of the time, Pallas kernels for 0%

commit v1 on v0

v1 whole, which is shorter than its diff:
```python
import functools

import jax
import jax.numpy as jnp
from jax import lax
from jax.experimental import pallas as pl
from jax.experimental.pallas import tpu as pltpu
from jax.sharding import PartitionSpec as P

soften_square = 0.01
block_step = 0.0625
LANES = 128
ROWS = 16
MESH = pl.DeviceIdType.MESH
NT = (((1,), (1,)), ((), ()))
VMEM = pl.BlockSpec(memory_space=pltpu.VMEM)
f32 = jnp.float32
bf16 = jnp.bfloat16


def split3(value):
    high = value.astype(bf16)
    rest = value - high.astype(f32)
    middle = rest.astype(bf16)
    low = (rest - middle.astype(f32)).astype(bf16)
    return high, middle, low


def sum3(stacked):
    return stacked[0:ROWS] + stacked[ROWS : 2 * ROWS] + stacked[2 * ROWS : 3 * ROWS]


def predict_rows(rows, now_time):
    delta = now_time - rows[12:13]
    pos, vel, acc, jerk = rows[0:3], rows[3:6], rows[6:9], rows[9:12]
    new_pos = pos + delta * (vel + delta * (acc / 2.0 + delta * jerk / 6.0))
    new_vel = vel + delta * (acc + delta * jerk / 2.0)
    return new_pos, new_vel


def gather_kernel(field_ref, ids_ref, out_ref, table, product):
    count = field_ref.shape[1]
    tiles = count // LANES
    for h in range(tiles):
        parts = split3(field_ref[:, h * LANES : (h + 1) * LANES])
        for p in range(3):
            table[p, h * ROWS : (h + 1) * ROWS, :] = parts[p].astype(f32)
    first = lax.axis_index("fld") * count
    width = out_ref.shape[2]

    def chunk(c, carry):
        local = ids_ref[c] - first
        high, low = local >> 7, local & (LANES - 1)
        hot = (lax.broadcasted_iota(jnp.int32, (LANES, width), 0) == low).astype(f32).astype(bf16)
        total = jnp.dot(table[0].astype(bf16), hot, preferred_element_type=f32)
        total += jnp.dot(table[1].astype(bf16), hot, preferred_element_type=f32)
        total += jnp.dot(table[2].astype(bf16), hot, preferred_element_type=f32)
        product[...] = total
        picked = jnp.zeros((ROWS, width), f32)
        for h in range(tiles):
            picked += jnp.where(high == h, product[h * ROWS : (h + 1) * ROWS, :], 0.0)
        out_ref[c] = picked
        return carry

    lax.fori_loop(0, out_ref.shape[0], chunk, 0)


def fetch_kernel(n, part_ref, out_ref, landing, gathered, send1, recv1, send2, recv2):
    act, me = lax.axis_index("act"), lax.axis_index("fld")
    barrier = pltpu.get_barrier_semaphore()
    for o in range(1, n):
        pl.semaphore_signal(barrier, inc=1, device_id=(act, lax.rem(me + o, n)), device_id_type=MESH)
    pl.semaphore_wait(barrier, n - 1)
    copies = []
    for o in range(1, n):
        peer = lax.rem(me + o, n)
        copies.append(pltpu.make_async_remote_copy(
            src_ref=part_ref.at[peer], dst_ref=landing.at[o], send_sem=send1.at[o], recv_sem=recv1.at[o],
            device_id=(act, peer), device_id_type=MESH))
        copies[-1].start()
    total = part_ref[me]
    for o in range(1, n):
        copies[o - 1].wait_recv()
        total += landing[o]
    gathered[me] = total
    again = []
    for o in range(1, n):
        peer = lax.rem(me + o, n)
        again.append(pltpu.make_async_remote_copy(
            src_ref=gathered.at[me], dst_ref=gathered.at[me], send_sem=send2.at[o], recv_sem=recv2.at[o],
            device_id=(act, peer), device_id_type=MESH))
        again[-1].start()
    for o in range(1, n):
        again[o - 1].wait_recv()
    for o in range(1, n):
        copies[o - 1].wait_send()
        again[o - 1].wait_send()
    width = part_ref.shape[2]
    for c in range(n):
        out_ref[:, c * width : (c + 1) * width] = gathered[c]


def update_field(field_in, field_out, values_ref, ids_ref, scaled):
    count = field_in.shape[1]
    tiles = count // LANES
    local = ids_ref[...] - lax.axis_index("fld") * count
    high, low = local >> 7, local & (LANES - 1)
    hot = (lax.broadcasted_iota(jnp.int32, (LANES, local.shape[1]), 0) == low).astype(f32).astype(bf16)
    parts = jnp.concatenate(split3(values_ref[...]), 0)
    for h in range(tiles):
        chosen = (high == h).astype(f32).astype(bf16)
        scaled[h * 3 * ROWS : (h + 1) * 3 * ROWS, :] = parts * chosen
    placed = lax.dot_general(scaled[...], hot, NT, preferred_element_type=f32)
    for h in range(tiles):
        fresh = sum3(placed[h * 3 * ROWS : (h + 1) * 3 * ROWS, :])
        old = field_in[:, h * LANES : (h + 1) * LANES]
        field_out[:, h * LANES : (h + 1) * LANES] = jnp.where(fresh[13:14] > 0.5, fresh, old)


def final_kernel(field_in, values_ref, ids_ref, out_ref, field, scaled):
    update_field(field_in, field, values_ref, ids_ref, scaled)
    out_ref[...] = field[0:12, :]


def pair_kernel(step, n, *refs):
    now_time = (step + 1) * block_step
    field_in, mass_ref, prev_in, column_ids = refs[:4]
    refs = refs[4:]
    values = refs[:step]
    ids = refs[step : 2 * step]
    refs = refs[2 * step :]
    sums_ref, prev_out = refs[:2]
    refs = refs[2:]
    if step:
        field = refs[0]
        points, columns, weight, second, potential, scaled = refs[1:]
        update_field(field_in, field, values[step - 1], ids[step - 1], scaled)
    else:
        field = field_in
        points, columns, weight, second, potential = refs
    count = field_in.shape[1]
    actives = prev_in.shape[1]
    previous = prev_in[...]
    for j in range(step):
        hot = (column_ids[...] == ids[j][...]).astype(f32).astype(bf16)
        parts = jnp.concatenate(split3(values[j][...]), 0)
        found = lax.dot_general(hot, parts, NT, preferred_element_type=f32)
        fresh = sum3(jnp.transpose(found))
        previous = jnp.where(fresh[13:14] > 0.5, fresh, previous)
    active_pos, active_vel = predict_rows(previous, now_time)
    pad2 = jnp.zeros((2, actives), f32)
    columns[...] = jnp.transpose(jnp.concatenate([active_pos, active_vel, pad2], 0))
    pos, vel = predict_rows(field[...], now_time)
    ones = jnp.ones((1, count), f32)
    both = jnp.concatenate([pos, vel, mass_ref[...], ones], 0)
    points[...] = both
    high = both.astype(bf16)
    low = (both - high.astype(f32)).astype(bf16)
    right = jnp.concatenate([high, low], 0)
    group = 16

    def one_group(i, carry):
        rows = pl.ds(pl.multiple_of(i * group, group), group)
        mine = [jnp.broadcast_to(columns[rows, r : r + 1], (group, LANES)) for r in range(6)]
        pot = jnp.zeros((group, LANES), f32)
        for c in range(count // LANES):
            at = slice(c * LANES, (c + 1) * LANES)
            sep = [points[r : r + 1, at] - mine[r] for r in range(3)]
            rel = [points[r : r + 1, at] - mine[r] for r in range(3, 6)]
            square = sep[0] * sep[0] + sep[1] * sep[1] + sep[2] * sep[2] + soften_square
            radial = sep[0] * rel[0] + sep[1] * rel[1] + sep[2] * rel[2]
            inverse = lax.rsqrt(square)
            inverse2 = inverse * inverse
            weighted = points[6:7, at] * inverse
            pot = pot + weighted
            w = weighted * inverse2
            weight[rows, at] = w.astype(bf16)
            second[rows, at] = (w * (inverse2 * radial)).astype(bf16)
        potential[rows, :] = pot
        return carry

    lax.fori_loop(0, actives // group, one_group, 0)
    first = jnp.transpose(lax.dot_general(weight[...], right, NT, preferred_element_type=f32))
    first = first[0:8] + first[8:16]
    other = jnp.transpose(lax.dot_general(second[...], right, NT, preferred_element_type=f32))
    other = other[0:8] + other[8:16]
    pot = -jnp.sum(jnp.transpose(potential[...]), axis=0, keepdims=True)
    pull = first[0:3] - active_pos * first[7:8]
    radial_part = other[0:3] - active_pos * other[7:8]
    jerk = first[3:6] - active_vel * first[7:8] - 3.0 * radial_part
    sums = jnp.concatenate([pull, jerk, pot, jnp.zeros((1, actives), f32)], 0)
    width = actives // n
    for c in range(n):
        sums_ref[c] = sums[:, c * width : (c + 1) * width]
        prev_out[c] = previous[:, c * width : (c + 1) * width]


def correct_rows(prev, total, now_time):
    h = now_time - prev[12:13]
    x0, v0, a0, j0 = prev[0:3], prev[3:6], prev[6:9], prev[9:12]
    a1, j1 = total[0:3], total[3:6]
    v1 = v0 + h * (a0 + a1) / 2.0 + h * h * (j0 - j1) / 12.0
    x1 = x0 + h * (v0 + v1) / 2.0 + h * h * (a0 - a1) / 12.0
    width = prev.shape[1]
    return jnp.concatenate([
        x1, v1, a1, j1, jnp.full((1, width), now_time, f32), jnp.ones((1, width), f32),
        total[6:7], jnp.zeros((1, width), f32)], 0)


def share_kernel(step, n_act, n, part_ref, prev_ref, out_ref, landing, gathered, send1, recv1, send2, recv2):
    act, me = lax.axis_index("act"), lax.axis_index("fld")
    devices = n_act * n
    index = act * n + me
    barrier = pltpu.get_barrier_semaphore()

    def place(o):
        other = lax.rem(index + o, devices)
        return (other // n, lax.rem(other, n))

    def greet(o, carry):
        pl.semaphore_signal(barrier, inc=1, device_id=place(o), device_id_type=MESH)
        return carry

    lax.fori_loop(1, devices, greet, 0)
    pl.semaphore_wait(barrier, devices - 1)
    copies = []
    for o in range(1, n):
        peer = lax.rem(me + o, n)
        copies.append(pltpu.make_async_remote_copy(
            src_ref=part_ref.at[peer], dst_ref=landing.at[o], send_sem=send1.at[o], recv_sem=recv1.at[o],
            device_id=(act, peer), device_id_type=MESH))
        copies[-1].start()
    total = part_ref[me]
    for o in range(1, n):
        copies[o - 1].wait_recv()
        total += landing[o]
    gathered[index] = correct_rows(prev_ref[me], total, (step + 1) * block_step)

    def copy(o):
        return pltpu.make_async_remote_copy(
            src_ref=gathered.at[index], dst_ref=gathered.at[index], send_sem=send2.at[o], recv_sem=recv2.at[o],
            device_id=place(o), device_id_type=MESH)

    def start(o, carry):
        copy(o).start()
        return carry

    def receive(o, carry):
        copy(o).wait_recv()
        return carry

    def sent(o, carry):
        copy(o).wait_send()
        return carry

    lax.fori_loop(1, devices, start, 0)
    lax.fori_loop(1, devices, receive, 0)
    width = part_ref.shape[2]
    for d in range(devices):
        out_ref[:, d * width : (d + 1) * width] = gathered[d]
    lax.fori_loop(1, devices, sent, 0)
    for o in range(1, n):
        copies[o - 1].wait_send()


def body(n_act, n_fld, star_state, star_times, masses, active_ids):
    count = star_state.shape[1]
    steps, listed = active_ids.shape
    actives = listed // n_act
    width = actives // n_fld
    devices = n_act * n_fld
    act = lax.axis_index("act")
    tiles = count // LANES
    field = jnp.concatenate([star_state, star_times[None], jnp.zeros((3, count), f32)], 0)
    mass = masses[None]
    mine = lax.dynamic_slice_in_dim(active_ids, act * actives, actives, 1)
    wide = steps * actives // n_fld
    params = functools.partial(pltpu.CompilerParams, vmem_limit_bytes=60 * 1024 * 1024)
    part = pl.pallas_call(
        gather_kernel,
        out_shape=jax.ShapeDtypeStruct((n_fld, ROWS, wide), f32),
        in_specs=[VMEM] * 2, out_specs=VMEM,
        scratch_shapes=[pltpu.VMEM((3, tiles * ROWS, LANES), f32), pltpu.VMEM((tiles * ROWS, wide), f32)],
        compiler_params=params(), name="gather",
    )(field, mine.reshape(n_fld, 1, wide))
    dma = pltpu.SemaphoreType.DMA
    fetched = pl.pallas_call(
        functools.partial(fetch_kernel, n_fld),
        out_shape=jax.ShapeDtypeStruct((ROWS, steps * actives), f32),
        in_specs=[VMEM], out_specs=VMEM,
        scratch_shapes=[pltpu.VMEM((n_fld, ROWS, wide), f32)] * 2 + [dma((n_fld,))] * 4,
        compiler_params=params(collective_id=0, has_side_effects=True), name="fetch",
    )(part)
    history, id_rows = [], []
    columns = mine.T
    for k in range(steps):
        outs = [jax.ShapeDtypeStruct((n_fld, 8, width), f32), jax.ShapeDtypeStruct((n_fld, ROWS, width), f32)]
        scratch = [
            pltpu.VMEM((8, count), f32), pltpu.VMEM((actives, 8), f32),
            pltpu.VMEM((actives, count), bf16), pltpu.VMEM((actives, count), bf16),
            pltpu.VMEM((actives, LANES), f32)]
        if k:
            outs.append(jax.ShapeDtypeStruct((ROWS, count), f32))
            scratch.append(pltpu.VMEM((tiles * 3 * ROWS, listed), bf16))
        results = pl.pallas_call(
            functools.partial(pair_kernel, k, n_fld),
            out_shape=outs, in_specs=[VMEM] * (4 + 2 * k), out_specs=[VMEM] * len(outs),
            scratch_shapes=scratch, compiler_params=params(), name=f"pairs{k}",
        )(field, mass, fetched[:, k * actives : (k + 1) * actives], columns[:, k : k + 1], *history, *id_rows)
        if k:
            field = results[2]
        values = pl.pallas_call(
            functools.partial(share_kernel, k, n_act, n_fld),
            out_shape=jax.ShapeDtypeStruct((ROWS, listed), f32),
            in_specs=[VMEM] * 2, out_specs=VMEM,
            scratch_shapes=[
                pltpu.VMEM((n_fld, 8, width), f32), pltpu.VMEM((devices, ROWS, width), f32),
                dma((n_fld,)), dma((n_fld,)), dma((devices,)), dma((devices,))],
            compiler_params=params(collective_id=k + 1, has_side_effects=True), name=f"share{k}",
        )(results[0], results[1])
        history.append(values)
        id_rows.append(active_ids[k : k + 1])
    final = pl.pallas_call(
        final_kernel,
        out_shape=jax.ShapeDtypeStruct((12, count), f32),
        in_specs=[VMEM] * 3, out_specs=VMEM,
        scratch_shapes=[pltpu.VMEM((ROWS, count), f32), pltpu.VMEM((tiles * 3 * ROWS, listed), bf16)],
        compiler_params=params(), name="final",
    )(field, history[-1], id_rows[-1])
    potentials = jnp.stack([lax.dynamic_slice_in_dim(v[14], act * actives, actives, 0) for v in history], 0)
    return final, potentials


def solution(mesh):
    in_specs = (P(None, "fld"), P("fld"), P("fld"), P())
    out_specs = (P(None, "fld"), P(None, "act"))
    run = functools.partial(body, mesh.shape["act"], mesh.shape["fld"])
    return jax.shard_map(run, mesh=mesh, in_specs=in_specs, out_specs=out_specs, check_vma=False)
```

time: 455 us -> 179 us (0.39); the launches traced: 447 us -> 178 us
  Pallas kernels: 0 us -> 166 us
  blocking collectives: 156 us -> 0 us
  local copies, waits for them, and re-layouts: 126 us -> 8.28 us
  other arithmetic: 95 us -> 2.35 us
  waiting for transfers between devices: 39.7 us -> 0 us
  between operations: 15 us -> 0.71 us
  matrix products: 13.2 us -> 0 us
    pallas_call x0 -> x11, Pallas kernels: none -> 166 us  [the longest x4 73.4 us: body(): pl.pallas_call(functools.partial(pair_kernel, k, n_fld), out_shape=outs,...]
    psum x4 -> x0, blocking collectives: 134 us -> none  [body(): totals = lax.psum(pair_terms, 'fld')]
    reduce_sum x33 -> x0, other arithmetic: 70.3 us -> none  [the longest x16 38.9 us: one_block(): pull = jnp.sum(weights * separation, axis=-1)]
    scatter x7 -> x0, local copies, waits for them, and re-layouts: 49.9 us -> none  [the longest x4 25.7 us: body(): current = current.at[:, target_rows].set(updates, mode='drop')]
    psum x1 -> x0, waiting for transfers between devices: 39.6 us -> none  [body(): fetched = lax.psum(picked_all, 'fld')]
    unnamed x74 -> x5, local copies, waits for them, and re-layouts: 31 us -> 0.15 us
    gather x3 -> x0, local copies, waits for them, and re-layouts: 26.3 us -> none  [the longest x1 20.6 us: body(): star_times[safe_all][None]]
    all_gather x4 -> x0, blocking collectives: 22.1 us -> none  [body(): updates = lax.all_gather(refreshed, 'act', axis=1, tiled=True)]
  transfers between devices with their start and end apart: 1 -> 0, of which waited for: 1 -> 0; matrix products, arithmetic and copies ran while one was open for 7% -> 0% of each run, Pallas kernels for 0% -> 0%
where the time goes in v1:
time: 179 us; the launch traced here: 178 us
  Pallas kernels  166 us (93%)
  local copies, waits for them, and re-layouts  8.28 us (5%)
  other arithmetic  2.35 us (1%)
    pallas_call x4, Pallas kernels, body(): pl.pallas_call(functools.partial(pair_kernel, k, n_fld), out_shape=outs,...  73.4 us
    pallas_call x4, Pallas kernels, body(): pl.pallas_call(functools.partial(share_kernel, k, n_act, n_fld), out_shap...  67.1 us
    pallas_call x1, Pallas kernels, body(): pl.pallas_call(functools.partial(fetch_kernel, n_fld), out_shape=jax.Shap...  17.1 us
    pallas_call x1, Pallas kernels, body(): pl.pallas_call(gather_kernel, out_shape=jax.ShapeDtypeStruct((n_fld, ROWS...  4.53 us
    pallas_call x1, Pallas kernels, body(): pl.pallas_call(final_kernel, out_shape=jax.ShapeDtypeStruct((12, count),...  4.2 us

profile of v1, /device:TPU:0, one launch (start us, length us, event | category | flops | bytes accessed | tf_op | source)
XLA Modules:
  0.0 177.7 jit_solution(12773311161758838578)
XLA Ops:
  0.6 0.7 constant_dynamic-slice_fusion.4
  1.3 0.6 reshape.16.ids_ref
  2.0 0.1 pad.6.clone
  2.1 1.7 maximum_maximum_fusion.field_ref.refs_0_
  3.8 4.5 %gather.1.part_ref = f32[8,16,256]{2,1,0:T(8,128)} custom-call(f32[16,4096]{1,0:T(8,128)} %maximum_maximum_fusion.field_ref.refs_0_, s32[8,1,256]{2,1,0:T(1,128)} %reshape.16.ids_ref), custom_call_target="tpu_custom_call" | custom-call | tf_op jit(solution)/shard_map/gather/pallas_call | solution.py:279
  8.3 17.1 %fetch.1 = f32[16,2048]{1,0:T(8,128)} custom-call(f32[8,16,256]{2,1,0:T(8,128)} %gather.1.part_ref), custom_call_target="tpu_custom_call" | custom-call | tf_op jit(solution)/shard_map/fetch/pallas_call | solution.py:287
  25.5 1.5 fusion.1
  26.9 0.1 copy.10
  27.1 1.2 fusion
  28.3 14.3 %pairs0.1 = (f32[8,8,64]{2,1,0:T(8,128)}, f32[8,16,64]{2,1,0:T(8,128)}) custom-call(f32[16,4096]{1,0:T(8,128)} %maximum_maximum_fusion.field_ref.refs_0_, f32[1,4096]{1,0:T(1,128)} %bitcast.4, f32[16,512]{1,0:T(8,128)} %get-tuple-element.30.refs_2_, s32[512,1]{1,0:T(8,128)} %get-tuple-element.26.refs_3_), custom_call_target="tpu_custom_call" | custom-call | tf_op jit(solution)/shard_map/pairs0/pallas_call | solution.py:305
  42.6 16.8 %share0.1.refs_4_ = f32[16,2048]{1,0:T(8,128)} custom-call(f32[8,8,64]{2,1,0:T(8,128)} %get-tuple-element.13.part_ref, f32[8,16,64]{2,1,0:T(8,128)} %get-tuple-element.14.prev_ref), custom_call_target="tpu_custom_call" | custom-call | tf_op jit(solution)/shard_map/share0/pallas_call | solution.py:312
  59.4 0.6 fusion.2
  60.0 21.9 %pairs1.1 = (f32[8,8,64]{2,1,0:T(8,128)}, f32[8,16,64]{2,1,0:T(8,128)}, f32[16,4096]{1,0:T(8,128)}) custom-call(f32[16,4096]{1,0:T(8,128)} %maximum_maximum_fusion.field_ref.refs_0_, f32[1,4096]{1,0:T(1,128)} %bitcast.5, f32[16,512]{1,0:T(8,128)} %get-tuple-element.31.refs_2_, s32[512,1]{1,0:T(8,128)} %get-tuple-element.27.refs_3_, ...), custom_call_target="tpu_custom_call" | custom-call | tf_op jit(solution)/shard_map/pairs1/pallas_call | solution.py:305
  82.0 17.1 %share1.1.refs_5_ = f32[16,2048]{1,0:T(8,128)} custom-call(f32[8,8,64]{2,1,0:T(8,128)} %get-tuple-element.16.part_ref, f32[8,16,64]{2,1,0:T(8,128)} %get-tuple-element.17.prev_ref), custom_call_target="tpu_custom_call" | custom-call | tf_op jit(solution)/shard_map/share1/pallas_call | solution.py:312
  99.1 0.8 slice.61
  99.9 0.8 slice.60
  100.8 18.3 %pairs2.1 = (f32[8,8,64]{2,1,0:T(8,128)}, f32[8,16,64]{2,1,0:T(8,128)}, f32[16,4096]{1,0:T(8,128)}) custom-call(f32[16,4096]{1,0:T(8,128)} %get-tuple-element.15.refs_0_, f32[1,4096]{1,0:T(1,128)} %bitcast.6, f32[16,512]{1,0:T(8,128)} %get-tuple-element.29.refs_2_, s32[512,1]{1,0:T(8,128)} %get-tuple-element.25.refs_3_, f32[16,2048]{1,0:T(8,128)} %share0.1.refs_4_, ...), custom_call_target="tpu_custom_call" | custom-call | tf_op jit(solution)/shard_map/pairs2/pallas_call | solution.py:305
  119.1 16.2 %share2.1.refs_6_ = f32[16,2048]{1,0:T(8,128)} custom-call(f32[8,8,64]{2,1,0:T(8,128)} %get-tuple-element.19.part_ref, f32[8,16,64]{2,1,0:T(8,128)} %get-tuple-element.20.prev_ref), custom_call_target="tpu_custom_call" | custom-call | tf_op jit(solution)/shard_map/share2/pallas_call | solution.py:312
  135.3 18.9 %pairs3.1 = (f32[8,8,64]{2,1,0:T(8,128)}, f32[8,16,64]{2,1,0:T(8,128)}, f32[16,4096]{1,0:T(8,128)}) custom-call(f32[16,4096]{1,0:T(8,128)} %get-tuple-element.18.refs_0_, f32[1,4096]{1,0:T(1,128)} %bitcast.7, f32[16,512]{1,0:T(8,128)} %get-tuple-element.28.refs_2_, s32[512,1]{1,0:T(8,128)} %get-tuple-element.24.refs_3_, f32[16,2048]{1,0:T(8,128)} %share0.1.refs_4_, ...), custom_call_target="tpu_custom_call" | custom-call | tf_op jit(solution)/shard_map/pairs3/pallas_call | solution.py:305
  154.2 17.0 %share3.1.values_ref = f32[16,2048]{1,0:T(8,128)} custom-call(f32[8,8,64]{2,1,0:T(8,128)} %get-tuple-element.22.part_ref, f32[8,16,64]{2,1,0:T(8,128)} %get-tuple-element.23.prev_ref), custom_call_target="tpu_custom_call" | custom-call | tf_op jit(solution)/shard_map/share3/pallas_call | solution.py:312
  171.2 0.8 slice.63
  172.1 0.8 slice.62
  172.9 0.6 pad_maximum_fusion
  173.5 4.2 %final.1 = f32[12,4096]{1,0:T(8,128)} custom-call(f32[16,4096]{1,0:T(8,128)} %get-tuple-element.21.field_in, f32[16,2048]{1,0:T(8,128)} %share3.1.values_ref, s32[1,2048]{1,0:T(1,128)} %get-tuple-element.32.ids_ref), custom_call_target="tpu_custom_call" | custom-call | tf_op jit(solution)/shard_map/final/pallas_call | solution.py:323
  (7 shorter events, 0.0 us)
Async XLA Ops:
  0.6 1.4 copy-start.1
  42.6 16.8 %copy-start = (s32[4,2048]{1,0:T(4,128)S(1)}, s32[4,2048]{1,0:T(4,128)}, u32[]{:S(2)}) copy-start(s32[4,2048]{1,0:T(4,128)} %param.7) | copy-start | bytes 98308

commit v2 on v1

v2 whole, which is shorter than its diff:
```python
import functools

import jax
import jax.numpy as jnp
from jax import lax
from jax.experimental import pallas as pl
from jax.experimental.pallas import tpu as pltpu
from jax.sharding import PartitionSpec as P

soften_square = 0.01
block_step = 0.0625
LANES = 128
CHUNK = 256
SHIFT = 8
ROWS = 16
MESH = pl.DeviceIdType.MESH
NT = (((1,), (1,)), ((), ()))
VMEM = pl.BlockSpec(memory_space=pltpu.VMEM)
f32 = jnp.float32
bf16 = jnp.bfloat16


def split3(value):
    high = value.astype(bf16)
    rest = value - high.astype(f32)
    middle = rest.astype(bf16)
    low = (rest - middle.astype(f32)).astype(bf16)
    return high, middle, low


def sum3(stacked):
    return stacked[0:ROWS] + stacked[ROWS : 2 * ROWS] + stacked[2 * ROWS : 3 * ROWS]


def predict_rows(rows, now_time):
    delta = now_time - rows[12:13]
    pos, vel, acc, jerk = rows[0:3], rows[3:6], rows[6:9], rows[9:12]
    new_pos = pos + delta * (vel + delta * (acc / 2.0 + delta * jerk / 6.0))
    new_vel = vel + delta * (acc + delta * jerk / 2.0)
    return new_pos, new_vel


def gather_kernel(state_ref, times_ref, ids_ref, out_ref, field_ref, table, product):
    count = state_ref.shape[1]
    tiles = count // CHUNK
    field_ref[...] = jnp.concatenate([state_ref[...], times_ref[...], jnp.zeros((3, count), f32)], 0)
    for h in range(tiles):
        parts = split3(field_ref[:, h * CHUNK : (h + 1) * CHUNK])
        for p in range(3):
            table[p, h * ROWS : (h + 1) * ROWS, :] = parts[p]
    first = lax.axis_index("fld") * count
    width = out_ref.shape[2]

    def chunk(c, carry):
        local = ids_ref[c] - first
        high, low = local >> SHIFT, local & (CHUNK - 1)
        hot = (lax.broadcasted_iota(jnp.int32, (CHUNK, width), 0) == low).astype(f32).astype(bf16)
        total = jnp.dot(table[0], hot, preferred_element_type=f32)
        total += jnp.dot(table[1], hot, preferred_element_type=f32)
        total += jnp.dot(table[2], hot, preferred_element_type=f32)
        product[...] = total
        picked = jnp.zeros((ROWS, width), f32)
        for h in range(tiles):
            picked += jnp.where(high == h, product[h * ROWS : (h + 1) * ROWS, :], 0.0)
        out_ref[c] = picked
        return carry

    lax.fori_loop(0, out_ref.shape[0], chunk, 0)


def fetch_kernel(n, part_ref, out_ref, landing, gathered, send1, recv1, send2, recv2):
    act, me = lax.axis_index("act"), lax.axis_index("fld")
    barrier = pltpu.get_barrier_semaphore()
    for o in range(1, n):
        pl.semaphore_signal(barrier, inc=1, device_id=(act, lax.rem(me + o, n)), device_id_type=MESH)
    pl.semaphore_wait(barrier, n - 1)
    copies = []
    for o in range(1, n):
        peer = lax.rem(me + o, n)
        copies.append(pltpu.make_async_remote_copy(
            src_ref=part_ref.at[peer], dst_ref=landing.at[o], send_sem=send1.at[o], recv_sem=recv1.at[o],
            device_id=(act, peer), device_id_type=MESH))
        copies[-1].start()
    total = part_ref[me]
    for o in range(1, n):
        copies[o - 1].wait_recv()
        total += landing[o]
    gathered[me] = total
    again = []
    for o in range(1, n):
        peer = lax.rem(me + o, n)
        again.append(pltpu.make_async_remote_copy(
            src_ref=gathered.at[me], dst_ref=gathered.at[me], send_sem=send2.at[o], recv_sem=recv2.at[o],
            device_id=(act, peer), device_id_type=MESH))
        again[-1].start()
    for o in range(1, n):
        again[o - 1].wait_recv()
    for o in range(1, n):
        copies[o - 1].wait_send()
        again[o - 1].wait_send()
    width = part_ref.shape[2]
    for c in range(n):
        out_ref[:, c * width : (c + 1) * width] = gathered[c]


def update_field(field_in, field_out, values_ref, ids, scaled):
    count = field_in.shape[1]
    tiles = count // CHUNK
    local = ids - lax.axis_index("fld") * count
    high, low = local >> SHIFT, local & (CHUNK - 1)
    hot = (lax.broadcasted_iota(jnp.int32, (CHUNK, local.shape[1]), 0) == low).astype(f32).astype(bf16)
    parts = jnp.concatenate(split3(values_ref[...]), 0)
    for h in range(tiles):
        chosen = (high == h).astype(f32).astype(bf16)
        scaled[h * 3 * ROWS : (h + 1) * 3 * ROWS, :] = parts * chosen
    placed = lax.dot_general(scaled[...], hot, NT, preferred_element_type=f32)
    for h in range(tiles):
        fresh = sum3(placed[h * 3 * ROWS : (h + 1) * 3 * ROWS, :])
        old = field_in[:, h * CHUNK : (h + 1) * CHUNK]
        field_out[:, h * CHUNK : (h + 1) * CHUNK] = jnp.where(fresh[13:14] > 0.5, fresh, old)


def final_kernel(field_in, values_ref, ids_ref, out_ref, field, scaled):
    update_field(field_in, field, values_ref, ids_ref[ids_ref.shape[0] - 1 :, :], scaled)
    out_ref[...] = field[0:12, :]


def pair_kernel(step, n, *refs):
    now_time = (step + 1) * block_step
    field_in, mass_ref, prev_in, column_ids, ids = refs[:5]
    refs = refs[5:]
    values = refs[:step]
    refs = refs[step:]
    sums_ref, prev_out = refs[:2]
    refs = refs[2:]
    if step:
        field = refs[0]
        points, right, mine, even, odd, sums, potential, scaled = refs[1:]
        update_field(field_in, field, values[step - 1], ids[step - 1 : step, :], scaled)
    else:
        field = field_in
        points, right, mine, even, odd, sums, potential = refs
    chunks = points.shape[0]
    parts_of, half = mine.shape[1], mine.shape[2]
    actives = parts_of * half
    previous = prev_in[:, step * actives : (step + 1) * actives]
    for j in range(step):
        hot = (column_ids[:, step : step + 1] == ids[j : j + 1, :]).astype(f32).astype(bf16)
        parts = jnp.concatenate(split3(values[j][...]), 0)
        found = lax.dot_general(hot, parts, NT, preferred_element_type=f32)
        fresh = sum3(jnp.transpose(found))
        previous = jnp.where(fresh[13:14] > 0.5, fresh, previous)
    active_pos, active_vel = predict_rows(previous, now_time)
    pad2 = jnp.zeros((2, actives), f32)
    columns = jnp.transpose(jnp.concatenate([active_pos, active_vel, pad2], 0))
    for r in range(6):
        for p in range(parts_of):
            mine[r, p] = jnp.broadcast_to(columns[p * half : (p + 1) * half, r : r + 1], (half, LANES))
    pos, vel = predict_rows(field[...], now_time)
    both = jnp.concatenate([pos, vel, mass_ref[...], jnp.ones((1, pos.shape[1]), f32)], 0)
    high = both.astype(bf16)
    low = (both - high.astype(f32)).astype(bf16)
    split = jnp.concatenate([high, low], 0)
    for c in range(chunks):
        points[c] = both[:, c * CHUNK : (c + 1) * CHUNK]
        right[c] = split[:, c * CHUNK : (c + 1) * CHUNK]
    group = 16
    sums[...] = jnp.zeros_like(sums)
    potential[...] = jnp.zeros_like(potential)
    odd[...] = jnp.zeros_like(odd)

    def fill(buffer, turn):
        p, c = turn // chunks, lax.rem(turn, chunks)
        for g in range(half // group):
            rows = slice(g * group, (g + 1) * group)
            pot = potential[p, rows, :]
            for t in range(CHUNK // LANES):
                at = slice(t * LANES, (t + 1) * LANES)
                sep = [points[c, r : r + 1, at] - mine[r, p, rows, :] for r in range(3)]
                rel = [points[c, r : r + 1, at] - mine[r, p, rows, :] for r in range(3, 6)]
                square = sep[0] * sep[0] + sep[1] * sep[1] + sep[2] * sep[2] + soften_square
                radial = sep[0] * rel[0] + sep[1] * rel[1] + sep[2] * rel[2]
                inverse = lax.rsqrt(square)
                inverse2 = inverse * inverse
                weighted = points[c, 6:7, at] * inverse
                pot = pot + weighted
                w = weighted * inverse2
                buffer[rows, at] = w.astype(bf16)
                buffer[half + g * group : half + (g + 1) * group, at] = (w * (inverse2 * radial)).astype(bf16)
            potential[p, rows, :] = pot

    def drain(buffer, turn):
        p, c = turn // chunks, lax.rem(turn, chunks)
        sums[p] += lax.dot_general(buffer[...], right[c], NT, preferred_element_type=f32)

    def two(i, carry):
        fill(even, 2 * i)
        drain(odd, jnp.maximum(2 * i - 1, 0))
        fill(odd, 2 * i + 1)
        drain(even, 2 * i)
        return carry

    turns = parts_of * chunks
    lax.fori_loop(0, turns // 2, two, 0)
    drain(odd, turns - 1)
    firsts, others, pots = [], [], []
    for p in range(parts_of):
        both = jnp.transpose(sums[p])
        both = both[0:8] + both[8:16]
        firsts.append(both[:, 0:half])
        others.append(both[:, half:])
        pots.append(-jnp.sum(jnp.transpose(potential[p]), axis=0, keepdims=True))
    first, other = jnp.concatenate(firsts, 1), jnp.concatenate(others, 1)
    pot = jnp.concatenate(pots, 1)
    pull = first[0:3] - active_pos * first[7:8]
    radial_part = other[0:3] - active_pos * other[7:8]
    jerk = first[3:6] - active_vel * first[7:8] - 3.0 * radial_part
    total = jnp.concatenate([pull, jerk, pot, jnp.zeros((1, actives), f32)], 0)
    width = actives // n
    for c in range(n):
        sums_ref[c] = total[:, c * width : (c + 1) * width]
        prev_out[c] = previous[:, c * width : (c + 1) * width]


def correct_rows(prev, total, now_time):
    h = now_time - prev[12:13]
    x0, v0, a0, j0 = prev[0:3], prev[3:6], prev[6:9], prev[9:12]
    a1, j1 = total[0:3], total[3:6]
    v1 = v0 + h * (a0 + a1) / 2.0 + h * h * (j0 - j1) / 12.0
    x1 = x0 + h * (v0 + v1) / 2.0 + h * h * (a0 - a1) / 12.0
    width = prev.shape[1]
    return jnp.concatenate([
        x1, v1, a1, j1, jnp.full((1, width), now_time, f32), jnp.ones((1, width), f32),
        total[6:7], jnp.zeros((1, width), f32)], 0)


def share_kernel(step, n_act, n, part_ref, prev_ref, out_ref, pot_ref, landing, gathered, send1, recv1, send2, recv2):
    act, me = lax.axis_index("act"), lax.axis_index("fld")
    devices = n_act * n
    index = act * n + me
    barrier = pltpu.get_barrier_semaphore()

    def place(o):
        other = lax.rem(index + o, devices)
        return (other // n, lax.rem(other, n))

    def greet(o, carry):
        pl.semaphore_signal(barrier, inc=1, device_id=place(o), device_id_type=MESH)
        return carry

    lax.fori_loop(1, devices, greet, 0)
    pl.semaphore_wait(barrier, devices - 1)
    copies = []
    for o in range(1, n):
        peer = lax.rem(me + o, n)
        copies.append(pltpu.make_async_remote_copy(
            src_ref=part_ref.at[peer], dst_ref=landing.at[o], send_sem=send1.at[o], recv_sem=recv1.at[o],
            device_id=(act, peer), device_id_type=MESH))
        copies[-1].start()
    total = part_ref[me]
    for o in range(1, n):
        copies[o - 1].wait_recv()
        total += landing[o]
    fresh = correct_rows(prev_ref[me], total, (step + 1) * block_step)
    gathered[index] = jnp.concatenate([fresh[0:8], fresh[8:16]], 1)

    def copy(o):
        return pltpu.make_async_remote_copy(
            src_ref=gathered.at[index], dst_ref=gathered.at[index], send_sem=send2.at[o], recv_sem=recv2.at[o],
            device_id=place(o), device_id_type=MESH)

    def start(o, carry):
        copy(o).start()
        return carry

    def receive(o, carry):
        copy(o).wait_recv()
        return carry

    def sent(o, carry):
        copy(o).wait_send()
        return carry

    lax.fori_loop(1, devices, start, 0)
    lax.fori_loop(1, devices, receive, 0)
    width = part_ref.shape[2]
    for d in range(devices):
        packed = gathered[d]
        out_ref[0:8, d * width : (d + 1) * width] = packed[:, 0:width]
        out_ref[8:16, d * width : (d + 1) * width] = packed[:, width:]
    for c in range(n):
        pot_ref[:, c * width : (c + 1) * width] = gathered[act * n + c][6:7, width:]
    lax.fori_loop(1, devices, sent, 0)
    for o in range(1, n):
        copies[o - 1].wait_send()


def body(n_act, n_fld, star_state, star_times, masses, active_ids):
    count = star_state.shape[1]
    steps, listed = active_ids.shape
    actives = listed // n_act
    width = actives // n_fld
    devices = n_act * n_fld
    act = lax.axis_index("act")
    tiles = count // CHUNK
    mine = lax.dynamic_slice_in_dim(active_ids, act * actives, actives, 1)
    wide = steps * actives // n_fld
    half = min(actives, 256)
    parts_of = actives // half
    params = functools.partial(pltpu.CompilerParams, vmem_limit_bytes=60 * 1024 * 1024)
    part, field = pl.pallas_call(
        gather_kernel,
        out_shape=[jax.ShapeDtypeStruct((n_fld, ROWS, wide), f32), jax.ShapeDtypeStruct((ROWS, count), f32)],
        in_specs=[VMEM] * 3, out_specs=[VMEM] * 2,
        scratch_shapes=[pltpu.VMEM((3, tiles * ROWS, CHUNK), bf16), pltpu.VMEM((tiles * ROWS, wide), f32)],
        compiler_params=params(), name="gather",
    )(star_state, star_times[None], mine.reshape(n_fld, 1, wide))
    dma = pltpu.SemaphoreType.DMA
    fetched = pl.pallas_call(
        functools.partial(fetch_kernel, n_fld),
        out_shape=jax.ShapeDtypeStruct((ROWS, steps * actives), f32),
        in_specs=[VMEM], out_specs=VMEM,
        scratch_shapes=[pltpu.VMEM((n_fld, ROWS, wide), f32)] * 2 + [dma((n_fld,))] * 4,
        compiler_params=params(collective_id=0, has_side_effects=True), name="fetch",
    )(part)
    history, pots = [], []
    columns = mine.T
    for k in range(steps):
        outs = [jax.ShapeDtypeStruct((n_fld, 8, width), f32), jax.ShapeDtypeStruct((n_fld, ROWS, width), f32)]
        scratch = [
            pltpu.VMEM((tiles, 8, CHUNK), f32), pltpu.VMEM((tiles, 16, CHUNK), bf16),
            pltpu.VMEM((6, parts_of, half, LANES), f32),
            pltpu.VMEM((2 * half, CHUNK), bf16), pltpu.VMEM((2 * half, CHUNK), bf16),
            pltpu.VMEM((parts_of, 2 * half, 16), f32), pltpu.VMEM((parts_of, half, LANES), f32)]
        if k:
            outs.append(jax.ShapeDtypeStruct((ROWS, count), f32))
            scratch.append(pltpu.VMEM((tiles * 3 * ROWS, listed), bf16))
        results = pl.pallas_call(
            functools.partial(pair_kernel, k, n_fld),
            out_shape=outs, in_specs=[VMEM] * (5 + k), out_specs=[VMEM] * len(outs),
            scratch_shapes=scratch, compiler_params=params(), name=f"pairs{k}",
        )(field, masses[None], fetched, columns, active_ids, *history)
        if k:
            field = results[2]
        values, pot = pl.pallas_call(
            functools.partial(share_kernel, k, n_act, n_fld),
            out_shape=[jax.ShapeDtypeStruct((ROWS, listed), f32), jax.ShapeDtypeStruct((1, actives), f32)],
            in_specs=[VMEM] * 2, out_specs=[VMEM] * 2,
            scratch_shapes=[
                pltpu.VMEM((n_fld, 8, width), f32), pltpu.VMEM((devices, 8, 2 * width), f32),
                dma((n_fld,)), dma((n_fld,)), dma((devices,)), dma((devices,))],
            compiler_params=params(collective_id=k + 1, has_side_effects=True), name=f"share{k}",
        )(results[0], results[1])
        history.append(values)
        pots.append(pot)
    final = pl.pallas_call(
        final_kernel,
        out_shape=jax.ShapeDtypeStruct((12, count), f32),
        in_specs=[VMEM] * 3, out_specs=VMEM,
        scratch_shapes=[pltpu.VMEM((ROWS, count), f32), pltpu.VMEM((tiles * 3 * ROWS, listed), bf16)],
        compiler_params=params(), name="final",
    )(field, history[-1], active_ids)
    return final, jnp.concatenate(pots, 0)


def solution(mesh):
    in_specs = (P(None, "fld"), P("fld"), P("fld"), P())
    out_specs = (P(None, "fld"), P(None, "act"))
    run = functools.partial(body, mesh.shape["act"], mesh.shape["fld"])
    return jax.shard_map(run, mesh=mesh, in_specs=in_specs, out_specs=out_specs, check_vma=False)
```

time: 179 us -> 151 us (0.84)
  Pallas kernels: 166 us -> 147 us
  local copies, waits for them, and re-layouts: 8.28 us -> 2.2 us
    pallas_call x4, Pallas kernels: 73.4 us -> 64.6 us  [body(): pl.pallas_call(functools.partial(pair_kernel, k, n_fld), out_shape=outs,...]
    pallas_call x4, Pallas kernels: 67.1 us -> 58.6 us  [body(): pl.pallas_call(functools.partial(share_kernel, k, n_act, n_fld), out_shap...]
    slice x7 -> x0, local copies, waits for them, and re-layouts: 6.72 us -> none  [the longest x4 3.39 us: body(): v[14]]
where the time goes in v2:
time: 151 us
  Pallas kernels  147 us (97%)
  local copies, waits for them, and re-layouts  2.2 us (1%)
    pallas_call x4, Pallas kernels, body(): pl.pallas_call(functools.partial(pair_kernel, k, n_fld), out_shape=outs,...  64.6 us
    pallas_call x4, Pallas kernels, body(): pl.pallas_call(functools.partial(share_kernel, k, n_act, n_fld), out_shap...  58.6 us
    pallas_call x1, Pallas kernels, body(): pl.pallas_call(functools.partial(fetch_kernel, n_fld), out_shape=jax.Shap...  17.1 us
    pallas_call x1, Pallas kernels, body(): pl.pallas_call(gather_kernel, out_shape=[jax.ShapeDtypeStruct((n_fld, ROW...  3.93 us
    pallas_call x1, Pallas kernels, body(): pl.pallas_call(final_kernel, out_shape=jax.ShapeDtypeStruct((12, count),...  3.08 us

profile of v2, /device:TPU:0, one launch (start us, length us, event | category | flops | bytes accessed | tf_op | source)
XLA Modules:
  0.0 150.9 jit_solution(10525996801281417350)
XLA Ops:
  0.6 0.7 constant_dynamic-slice_fusion
  1.3 0.6 reshape.8.ids_ref
  2.0 0.9 copy.10
  2.8 3.9 %gather.1 = (f32[8,16,256]{2,1,0:T(8,128)}, f32[16,4096]{1,0:T(8,128)}) custom-call(f32[12,4096]{1,0:T(8,128)} %state_ref.1, f32[1,4096]{1,0:T(1,128)} %bitcast.11, s32[8,1,256]{2,1,0:T(1,128)} %reshape.8.ids_ref), custom_call_target="tpu_custom_call" | custom-call | tf_op jit(solution)/shard_map/gather/pallas_call | solution.py:311
  6.7 17.1 %fetch.1.refs_2_ = f32[16,2048]{1,0:T(8,128)} custom-call(f32[8,16,256]{2,1,0:T(8,128)} %get-tuple-element.24.part_ref), custom_call_target="tpu_custom_call" | custom-call | tf_op jit(solution)/shard_map/fetch/pallas_call | solution.py:319
  23.9 14.1 %pairs0.1 = (f32[8,8,64]{2,1,0:T(8,128)}, f32[8,16,64]{2,1,0:T(8,128)}) custom-call(f32[16,4096]{1,0:T(8,128)} %get-tuple-element.23.refs_0_, f32[1,4096]{1,0:T(1,128)} %bitcast.7, f32[16,2048]{1,0:T(8,128)} %fetch.1.refs_2_, s32[512,4]{1,0:T(8,128)} %bitcast.3, s32[4,2048]{1,0:T(4,128)} %ids_ref.1), custom_call_target="tpu_custom_call" | custom-call | tf_op jit(solution)/shard_map/pairs0/pallas_call | solution.py:338
  38.0 14.1 %share0.1 = (f32[16,2048]{1,0:T(8,128)}, f32[1,512]{1,0:T(1,128)}) custom-call(f32[8,8,64]{2,1,0:T(8,128)} %get-tuple-element.25.part_ref, f32[8,16,64]{2,1,0:T(8,128)} %get-tuple-element.26.prev_ref), custom_call_target="tpu_custom_call" | custom-call | tf_op jit(solution)/shard_map/share0/pallas_call | solution.py:345
  52.1 16.0 %pairs1.1 = (f32[8,8,64]{2,1,0:T(8,128)}, f32[8,16,64]{2,1,0:T(8,128)}, f32[16,4096]{1,0:T(8,128)}) custom-call(f32[16,4096]{1,0:T(8,128)} %get-tuple-element.23.refs_0_, f32[1,4096]{1,0:T(1,128)} %bitcast.8, f32[16,2048]{1,0:T(8,128)} %fetch.1.refs_2_, s32[512,4]{1,0:T(8,128)} %bitcast.4, s32[4,2048]{1,0:T(4,128)} %ids_ref.1, ...), custom_call_target="tpu_custom_call" | custom-call | tf_op jit(solution)/shard_map/pairs1/pallas_call | solution.py:338
  68.0 15.4 %share1.1 = (f32[16,2048]{1,0:T(8,128)}, f32[1,512]{1,0:T(1,128)}) custom-call(f32[8,8,64]{2,1,0:T(8,128)} %get-tuple-element.29.part_ref, f32[8,16,64]{2,1,0:T(8,128)} %get-tuple-element.30.prev_ref), custom_call_target="tpu_custom_call" | custom-call | tf_op jit(solution)/shard_map/share1/pallas_call | solution.py:345
  83.4 17.0 %pairs2.1 = (f32[8,8,64]{2,1,0:T(8,128)}, f32[8,16,64]{2,1,0:T(8,128)}, f32[16,4096]{1,0:T(8,128)}) custom-call(f32[16,4096]{1,0:T(8,128)} %get-tuple-element.28.refs_0_, f32[1,4096]{1,0:T(1,128)} %bitcast.9, f32[16,2048]{1,0:T(8,128)} %fetch.1.refs_2_, s32[512,4]{1,0:T(8,128)} %bitcast.5, s32[4,2048]{1,0:T(4,128)} %ids_ref.1, ...), custom_call_target="tpu_custom_call" | custom-call | tf_op jit(solution)/shard_map/pairs2/pallas_call | solution.py:338
  100.4 13.8 %share2.1 = (f32[16,2048]{1,0:T(8,128)}, f32[1,512]{1,0:T(1,128)}) custom-call(f32[8,8,64]{2,1,0:T(8,128)} %get-tuple-element.33.part_ref, f32[8,16,64]{2,1,0:T(8,128)} %get-tuple-element.34.prev_ref), custom_call_target="tpu_custom_call" | custom-call | tf_op jit(solution)/shard_map/share2/pallas_call | solution.py:345
  114.2 17.5 %pairs3.1 = (f32[8,8,64]{2,1,0:T(8,128)}, f32[8,16,64]{2,1,0:T(8,128)}, f32[16,4096]{1,0:T(8,128)}) custom-call(f32[16,4096]{1,0:T(8,128)} %get-tuple-element.32.refs_0_, f32[1,4096]{1,0:T(1,128)} %bitcast.10, f32[16,2048]{1,0:T(8,128)} %fetch.1.refs_2_, s32[512,4]{1,0:T(8,128)} %bitcast.6, s32[4,2048]{1,0:T(4,128)} %ids_ref.1, ...), custom_call_target="tpu_custom_call" | custom-call | tf_op jit(solution)/shard_map/pairs3/pallas_call | solution.py:338
  131.8 15.3 %share3.1 = (f32[16,2048]{1,0:T(8,128)}, f32[1,512]{1,0:T(1,128)}) custom-call(f32[8,8,64]{2,1,0:T(8,128)} %get-tuple-element.37.part_ref, f32[8,16,64]{2,1,0:T(8,128)} %get-tuple-element.38.prev_ref), custom_call_target="tpu_custom_call" | custom-call | tf_op jit(solution)/shard_map/share3/pallas_call | solution.py:345
  147.1 0.0 copy-start
  147.1 0.0 copy-start.1
  147.1 0.0 copy-start.2
  147.1 0.0 copy-start.3
  147.2 3.1 %final.1 = f32[12,4096]{1,0:T(8,128)} custom-call(f32[16,4096]{1,0:T(8,128)} %get-tuple-element.36.field_in, f32[16,2048]{1,0:T(8,128)} %get-tuple-element.39.values_ref, s32[4,2048]{1,0:T(4,128)} %ids_ref.1), custom_call_target="tpu_custom_call" | custom-call | tf_op jit(solution)/shard_map/final/pallas_call | solution.py:356
  150.2 0.0 copy-done
  150.2 0.0 copy-done.1
  150.2 0.0 copy-done.2
  150.2 0.0 copy-done.3
  150.2 0.6 pad_maximum_fusion
Async XLA Ops:
  147.1 3.1 %copy-start = (f32[1,512]{1,0:T(1,128)S(1)}, f32[1,512]{1,0:T(1,128)}, u32[]{:S(2)}) copy-start(f32[1,512]{1,0:T(1,128)} %get-tuple-element.40) | copy-start | bytes 6148
  147.1 3.1 %copy-start.1 = (f32[1,512]{1,0:T(1,128)S(1)}, f32[1,512]{1,0:T(1,128)}, u32[]{:S(2)}) copy-start(f32[1,512]{1,0:T(1,128)} %get-tuple-element.41) | copy-start | bytes 6148
  147.1 3.1 %copy-start.2 = (f32[1,512]{1,0:T(1,128)S(1)}, f32[1,512]{1,0:T(1,128)}, u32[]{:S(2)}) copy-start(f32[1,512]{1,0:T(1,128)} %get-tuple-element.42) | copy-start | bytes 6148
  147.1 3.1 %copy-start.3 = (f32[1,512]{1,0:T(1,128)S(1)}, f32[1,512]{1,0:T(1,128)}, u32[]{:S(2)}) copy-start(f32[1,512]{1,0:T(1,128)} %get-tuple-element.43) | copy-start | bytes 6148

commit v3 on v2

--- a/solution.py
+++ b/solution.py
@@ -193,14 +193,15 @@
         p, c = turn // chunks, lax.rem(turn, chunks)
         sums[p] += lax.dot_general(buffer[...], right[c], NT, preferred_element_type=f32)
 
+    turns = parts_of * chunks
+
     def two(i, carry):
         fill(even, 2 * i)
-        drain(odd, jnp.maximum(2 * i - 1, 0))
+        drain(odd, lax.rem(2 * i - 1 + turns, turns))
         fill(odd, 2 * i + 1)
         drain(even, 2 * i)
         return carry
 
-    turns = parts_of * chunks
     lax.fori_loop(0, turns // 2, two, 0)
     drain(odd, turns - 1)
     firsts, others, pots = [], [], []
@@ -234,7 +235,7 @@
         total[6:7], jnp.zeros((1, width), f32)], 0)
 
 
-def share_kernel(step, n_act, n, part_ref, prev_ref, out_ref, pot_ref, landing, gathered, send1, recv1, send2, recv2):
+def share_rows(compute, step, n_act, n, part_ref, prev_ref, out_ref, pot_ref, landing, gathered, send1, recv1, send2, recv2):
     act, me = lax.axis_index("act"), lax.axis_index("fld")
     devices = n_act * n
     index = act * n + me
@@ -249,6 +250,7 @@
         return carry
 
     lax.fori_loop(1, devices, greet, 0)
+    compute()
     pl.semaphore_wait(barrier, devices - 1)
     copies = []
     for o in range(1, n):
@@ -293,6 +295,19 @@
     lax.fori_loop(1, devices, sent, 0)
     for o in range(1, n):
         copies[o - 1].wait_send()
+
+
+def step_kernel(step, n_act, n, *refs):
+    inputs, refs = refs[: 5 + step], refs[5 + step :]
+    out_ref, pot_ref = refs[:2]
+    kept, refs = refs[2 : 2 + (step > 0)], refs[2 + (step > 0) :]
+    part, prev = refs[:2]
+    exchange, scratch = refs[2:8], refs[8:]
+
+    def compute():
+        pair_kernel(step, n, *inputs, part, prev, *kept, *scratch)
+
+    share_rows(compute, step, n_act, n, part, prev, out_ref, pot_ref, *exchange)
 
 
 def body(n_act, n_fld, star_state, star_times, masses, active_ids):
@@ -326,8 +341,11 @@
     history, pots = [], []
     columns = mine.T
     for k in range(steps):
-        outs = [jax.ShapeDtypeStruct((n_fld, 8, width), f32), jax.ShapeDtypeStruct((n_fld, ROWS, width), f32)]
+        outs = [jax.ShapeDtypeStruct((ROWS, listed), f32), jax.ShapeDtypeStruct((1, actives), f32)]
         scratch = [
+            pltpu.VMEM((n_fld, 8, width), f32), pltpu.VMEM((n_fld, ROWS, width), f32),
+            pltpu.VMEM((n_fld, 8, width), f32), pltpu.VMEM((devices, 8, 2 * width), f32),
+            dma((n_fld,)), dma((n_fld,)), dma((devices,)), dma((devices,)),
             pltpu.VMEM((tiles, 8, CHUNK), f32), pltpu.VMEM((tiles, 16, CHUNK), bf16),
             pltpu.VMEM((6, parts_of, half, LANES), f32),
             pltpu.VMEM((2 * half, CHUNK), bf16), pltpu.VMEM((2 * half, CHUNK), bf16),
@@ -336,21 +354,14 @@
             outs.append(jax.ShapeDtypeStruct((ROWS, count), f32))
             scratch.append(pltpu.VMEM((tiles * 3 * ROWS, listed), bf16))
         results = pl.pallas_call(
-            functools.partial(pair_kernel, k, n_fld),
+            functools.partial(step_kernel, k, n_act, n_fld),
             out_shape=outs, in_specs=[VMEM] * (5 + k), out_specs=[VMEM] * len(outs),
-            scratch_shapes=scratch, compiler_params=params(), name=f"pairs{k}",
+            scratch_shapes=scratch, name=f"step{k}",
+            compiler_params=params(collective_id=k + 1, has_side_effects=True),
         )(field, masses[None], fetched, columns, active_ids, *history)
+        values, pot = results[:2]
         if k:
             field = results[2]
-        values, pot = pl.pallas_call(
-            functools.partial(share_kernel, k, n_act, n_fld),
-            out_shape=[jax.ShapeDtypeStruct((ROWS, listed), f32), jax.ShapeDtypeStruct((1, actives), f32)],
-            in_specs=[VMEM] * 2, out_specs=[VMEM] * 2,
-            scratch_shapes=[
-                pltpu.VMEM((n_fld, 8, width), f32), pltpu.VMEM((devices, 8, 2 * width), f32),
-                dma((n_fld,)), dma((n_fld,)), dma((devices,)), dma((devices,))],
-            compiler_params=params(collective_id=k + 1, has_side_effects=True), name=f"share{k}",
-        )(results[0], results[1])
         history.append(values)
         pots.append(pot)
     final = pl.pallas_call(

time: 151 us -> 134 us (0.89)
  Pallas kernels: 147 us -> 131 us
    pallas_call x8 -> x4, Pallas kernels: 123 us -> 107 us  [body(): pl.pallas_call(functools.partial(step_kernel, k, n_act, n_fld), out_shape...]
where the time goes in v3:
time: 134 us
  Pallas kernels  131 us (98%)
  local copies, waits for them, and re-layouts  2.19 us (2%)
    pallas_call x4, Pallas kernels, body(): pl.pallas_call(functools.partial(step_kernel, k, n_act, n_fld), out_shape...  107 us
    pallas_call x1, Pallas kernels, body(): pl.pallas_call(functools.partial(fetch_kernel, n_fld), out_shape=jax.Shap...  17.1 us
    pallas_call x1, Pallas kernels, body(): pl.pallas_call(gather_kernel, out_shape=[jax.ShapeDtypeStruct((n_fld, ROW...  3.9 us
    pallas_call x1, Pallas kernels, body(): pl.pallas_call(final_kernel, out_shape=jax.ShapeDtypeStruct((12, count),...  3.08 us

profile of v3, /device:TPU:0, one launch (start us, length us, event | category | flops | bytes accessed | tf_op | source)
XLA Modules:
  0.0 134.2 jit_solution(10865217796533032675)
XLA Ops:
  0.6 0.7 constant_dynamic-slice_fusion
  1.3 0.6 reshape.8.ids_ref
  2.0 0.8 copy.10
  2.8 3.9 %gather.1 = (f32[8,16,256]{2,1,0:T(8,128)}, f32[16,4096]{1,0:T(8,128)}) custom-call(f32[12,4096]{1,0:T(8,128)} %state_ref.1, f32[1,4096]{1,0:T(1,128)} %bitcast.11, s32[8,1,256]{2,1,0:T(1,128)} %reshape.8.ids_ref), custom_call_target="tpu_custom_call" | custom-call | tf_op jit(solution)/shard_map/gather/pallas_call | solution.py:326
  6.7 17.1 %fetch.1.refs_2_ = f32[16,2048]{1,0:T(8,128)} custom-call(f32[8,16,256]{2,1,0:T(8,128)} %get-tuple-element.16.part_ref), custom_call_target="tpu_custom_call" | custom-call | tf_op jit(solution)/shard_map/fetch/pallas_call | solution.py:334
  23.9 24.9 %step0.1 = (f32[16,2048]{1,0:T(8,128)}, f32[1,512]{1,0:T(1,128)}) custom-call(f32[16,4096]{1,0:T(8,128)} %get-tuple-element.15.refs_0_, f32[1,4096]{1,0:T(1,128)} %bitcast.7, f32[16,2048]{1,0:T(8,128)} %fetch.1.refs_2_, s32[512,4]{1,0:T(8,128)} %bitcast.3, s32[4,2048]{1,0:T(4,128)} %ids_ref.1), custom_call_target="tpu_custom_call" | custom-call | tf_op jit(solution)/shard_map/step0/pallas_call | solution.py:356
  48.8 26.2 %step1.1 = (f32[16,2048]{1,0:T(8,128)}, f32[1,512]{1,0:T(1,128)}, f32[16,4096]{1,0:T(8,128)}) custom-call(f32[16,4096]{1,0:T(8,128)} %get-tuple-element.15.refs_0_, f32[1,4096]{1,0:T(1,128)} %bitcast.8, f32[16,2048]{1,0:T(8,128)} %fetch.1.refs_2_, s32[512,4]{1,0:T(8,128)} %bitcast.4, s32[4,2048]{1,0:T(4,128)} %ids_ref.1, f32[16,2048]{1,0:T(8,128)} %get-tuple-element.17.refs_5_), custom_call_target="tpu_custom_call" | custom-call | tf_op jit(solution)/shard_map/step1/pallas_call | solution.py:356
  75.0 27.4 %step2.1 = (f32[16,2048]{1,0:T(8,128)}, f32[1,512]{1,0:T(1,128)}, f32[16,4096]{1,0:T(8,128)}) custom-call(f32[16,4096]{1,0:T(8,128)} %get-tuple-element.18.refs_0_, f32[1,4096]{1,0:T(1,128)} %bitcast.9, f32[16,2048]{1,0:T(8,128)} %fetch.1.refs_2_, s32[512,4]{1,0:T(8,128)} %bitcast.5, s32[4,2048]{1,0:T(4,128)} %ids_ref.1, ...), custom_call_target="tpu_custom_call" | custom-call | tf_op jit(solution)/shard_map/step2/pallas_call | solution.py:356
  102.4 28.0 %step3.1 = (f32[16,2048]{1,0:T(8,128)}, f32[1,512]{1,0:T(1,128)}, f32[16,4096]{1,0:T(8,128)}) custom-call(f32[16,4096]{1,0:T(8,128)} %get-tuple-element.20.refs_0_, f32[1,4096]{1,0:T(1,128)} %bitcast.10, f32[16,2048]{1,0:T(8,128)} %fetch.1.refs_2_, s32[512,4]{1,0:T(8,128)} %bitcast.6, s32[4,2048]{1,0:T(4,128)} %ids_ref.1, ...), custom_call_target="tpu_custom_call" | custom-call | tf_op jit(solution)/shard_map/step3/pallas_call | solution.py:356
  130.4 0.0 copy-start
  130.4 0.0 copy-start.1
  130.5 0.0 copy-start.2
  130.5 0.0 copy-start.3
  130.5 3.1 %final.1 = f32[12,4096]{1,0:T(8,128)} custom-call(f32[16,4096]{1,0:T(8,128)} %get-tuple-element.22.field_in, f32[16,2048]{1,0:T(8,128)} %get-tuple-element.23.values_ref, s32[4,2048]{1,0:T(4,128)} %ids_ref.1), custom_call_target="tpu_custom_call" | custom-call | tf_op jit(solution)/shard_map/final/pallas_call | solution.py:367
  133.6 0.0 copy-done
  133.6 0.0 copy-done.1
  133.6 0.0 copy-done.2
  133.6 0.0 copy-done.3
  133.6 0.6 pad_maximum_fusion
Async XLA Ops:
  130.4 3.1 %copy-start = (f32[1,512]{1,0:T(1,128)S(1)}, f32[1,512]{1,0:T(1,128)}, u32[]{:S(2)}) copy-start(f32[1,512]{1,0:T(1,128)} %get-tuple-element.24) | copy-start | bytes 6148
  130.4 3.1 %copy-start.1 = (f32[1,512]{1,0:T(1,128)S(1)}, f32[1,512]{1,0:T(1,128)}, u32[]{:S(2)}) copy-start(f32[1,512]{1,0:T(1,128)} %get-tuple-element.25) | copy-start | bytes 6148
  130.5 3.1 %copy-start.2 = (f32[1,512]{1,0:T(1,128)S(1)}, f32[1,512]{1,0:T(1,128)}, u32[]{:S(2)}) copy-start(f32[1,512]{1,0:T(1,128)} %get-tuple-element.26) | copy-start | bytes 6148
  130.5 3.1 %copy-start.3 = (f32[1,512]{1,0:T(1,128)S(1)}, f32[1,512]{1,0:T(1,128)}, u32[]{:S(2)}) copy-start(f32[1,512]{1,0:T(1,128)} %get-tuple-element.27) | copy-start | bytes 6148
